TPU v7x, 32 devices: a whole 2x2x4 slice. The times are simulated.
32 devices in a mesh: mem: 4 (over x, core), lon: 8 (over z, y).
Axes of the slice: x: 2, y: 2, z: 4, core: 2. Of those that a mesh axis runs over, the one named last changes fastest.
Arguments:
- controls: bfloat16 [2048, 32, 1024], P('lon', 'mem'), may hold values from -6 to 6
- perturbations: bfloat16 [2048, 32, 1024], P(None, 'mem', 'lon'), may hold values from -0.59765625 to 0.59765625
- lat_factor: bfloat16 [1024, 1024], P('mem'), may hold values from -0.09375 to 0.09375
- lon_factor: bfloat16 [2048, 2048], P('mem'), may hold values from -0.0625 to 0.0625
- obs_index: int32 [4, 8, 32768], P('mem', 'lon'), may hold values from 0 to 65535
- obs_weight: float32 [4, 8, 32768], P('mem', 'lon'), may hold values from 1 to 30
- obs_count: int32 [4, 8], P('mem', 'lon'), may hold values from 8193 to 32768, as said below
Outputs:
- hessian_product: float32 [2048, 32, 1024], P('lon', 'mem')
Inputs may be any that keep to these rules, and one draw needn't show every extreme that they name: `obs_index`: several slots may name one grid point; grid points are numbered with latitude fastest within a tile of 512 by 128. `obs_count`: slots 0 to count - 1 of a tile are in use; some tile uses all 32768 slots.
All inputs are finite; a program needn't handle non-finite values.
Results may differ from a plain program's by a relative error of at most 0.008.
Values may be sent and summed in bfloat16 or wider, within the bound.
No kernel may reach another device: no remote copies, remote signals or barrier semaphores. Data moves between devices by JAX's collectives and lax.ppermute only.
A program may use at most 128 MiB of HBM per device.

v0:
```python
import jax
import jax.numpy as jnp
from jax import lax
from jax.sharding import PartitionSpec as P


def observe(grid_field, index_rows, weight_rows, count_rows):
    tile_count, slot_count = index_rows.shape
    flattened = grid_field.reshape(-1)
    tile_cells = flattened.shape[0] // tile_count
    where_at = index_rows + (jnp.arange(tile_count, dtype=jnp.int32) * tile_cells)[:, None]
    in_use = jnp.arange(slot_count, dtype=jnp.int32)[None, :] < count_rows[:, None]
    picked = flattened[where_at]
    values = jnp.where(in_use, weight_rows * picked, jnp.zeros_like(picked))
    return (
        jnp.zeros_like(flattened)
        .at[where_at.reshape(-1)]
        .add(values.reshape(-1))
        .reshape(grid_field.shape)
    )


def local(controls, perturbations, lat_factor, lon_factor, obs_index, obs_weight, obs_count):
    lon_dev, mem_dev, lat_all = controls.shape
    lat_full = lax.all_gather(lat_factor, "mem", axis=0, tiled=True)
    control_rows = controls.reshape(lon_dev * mem_dev, lat_all)
    banded = (
        control_rows.astype(jnp.float32)
        + lax.dot_general(
            control_rows, lat_full, (((1,), (1,)), ((), ())), preferred_element_type=jnp.float32
        )
    ).astype(jnp.bfloat16)
    moved = lax.all_to_all(
        banded.reshape(lon_dev, mem_dev, lat_all), "lon", split_axis=2, concat_axis=0, tiled=True
    )
    lon_all, _, lat_band = moved.shape
    columns = moved.reshape(lon_all, mem_dev * lat_band)
    lon_full = lax.all_gather(lon_factor, "mem", axis=0, tiled=True)
    spread_fwd = jnp.dot(lon_full, columns, preferred_element_type=jnp.float32)
    localized = columns.astype(jnp.float32) + spread_fwd
    weighted_fwd = (
        perturbations.reshape(lon_all, mem_dev * lat_band).astype(jnp.float32) * localized
    )
    partial_sum = jnp.sum(weighted_fwd.reshape(lon_all, mem_dev, lat_band), axis=1)
    slot_count = obs_index.shape[-1]
    tile_sum = lax.psum_scatter(partial_sum, "mem", scatter_dimension=0, tiled=True)
    grad_tile = observe(
        tile_sum,
        obs_index.reshape(-1, slot_count),
        obs_weight.reshape(-1, slot_count),
        obs_count.reshape(-1),
    ).astype(jnp.bfloat16)
    gradient = lax.all_gather(grad_tile, "mem", axis=0, tiled=True)
    weighted = (
        (perturbations.astype(jnp.float32) * gradient.astype(jnp.float32)[:, None, :])
        .astype(jnp.bfloat16)
        .reshape(lon_all, mem_dev * lat_band)
    )
    spread_back = lax.dot_general(
        lon_full, weighted, (((0,), (0,)), ((), ())), preferred_element_type=jnp.float32
    )
    spread = (
        (weighted.astype(jnp.float32) + spread_back)
        .astype(jnp.bfloat16)
        .reshape(lon_all, mem_dev, lat_band)
    )
    returned = lax.all_to_all(spread, "lon", split_axis=0, concat_axis=2, tiled=True)
    back_rows = returned.reshape(lon_dev * mem_dev, lat_all)
    result = (
        control_rows.astype(jnp.float32)
        + back_rows.astype(jnp.float32)
        + jnp.dot(back_rows, lat_full, preferred_element_type=jnp.float32)
    )
    return result.reshape(lon_dev, mem_dev, lat_all)


def solution(mesh):
    in_specs = (
        P("lon", "mem", None),
        P(None, "mem", "lon"),
        P("mem", None),
        P("mem", None),
        P("mem", "lon", None),
        P("mem", "lon", None),
        P("mem", "lon"),
    )
    out_specs = P("lon", "mem", None)
    return jax.shard_map(local, mesh=mesh, in_specs=in_specs, out_specs=out_specs, check_vma=False)
```

profile of v0, /device:TPU:0, one launch (start us, length us, event | category | flops | bytes accessed | tf_op | source)
XLA Modules:
  0.0 709.8 jit_solution(16194023989570546402)
XLA Ops:
  6.5 0.7 all-gather.3.cloned.1.call-update
  7.3 0.7 all-gather.5.cloned.1.call-update
  8.0 26.2 %all-gather.3.cloned.1.call-done = bf16[1024,1024]{1,0:T(8,128)(2,1)} async-done(((bf16[256,1024]{1,0:T(8,128)(2,1)}), bf16[1024,1024]{1,0:T(8,128)(2,1)}) %all-gather.3.cloned.1.call-update) | async-done | bytes 2097168 | tf_op jit(solution)/shard_map/all_gather | solution.py:25
  34.2 10.8 %fusion.5 = bf16[256,8,1024]{2,1,0:T(8,128)(2,1)} fusion(bf16[256,8,1024]{2,1,0:T(8,128)(2,1)} %param.7, bf16[1024,1024]{1,0:T(8,128)(2,1)} %all-gather.3.cloned.1.call-done), kind=kOutput, calls=%fused_computation.12 | convolution fusion | flops 4301258752 | bytes 10485760 | tf_op jit(solution)/shard_map/dot_general | solution.py:29
  45.0 7.5 %copy.30 = bf16[256,8,1024]{0,1,2:T(8,128)(2,1)} copy(bf16[256,8,1024]{2,1,0:T(8,128)(2,1)} %fusion.5) | data formatting | bytes 8388608 | tf_op jit(solution)/shard_map/reshape | solution.py:34
  52.4 5.6 all-to-all-start
  58.0 0.2 reduce-scatter.2.cloned.1.call-start
  58.2 7.7 %copy.29 = f32[2048,8,128]{0,2,1:T(8,128)} copy(bf16[2048,8,128]{2,1,0:T(8,128)(2,1)} %param.8) | data formatting | bytes 12582912 | tf_op jit(solution)/shard_map/convert_element_type | solution.py:55
  66.1 85.6 %all-to-all-done = bf16[256,8,1024]{0,1,2:T(8,128)(2,1)} async-done(((bf16[256,8,1024]{0,1,2:T(8,128)(2,1)}), bf16[256,8,1024]{0,1,2:T(8,128)(2,1)}, u32[]{:S(2)}, u32[]{:S(2)}) %all-to-all-start) | async-done | bytes 4194336 | tf_op jit(solution)/shard_map/all_to_all | solution.py:33
  151.7 4.6 copy.31
  156.2 3.4 copy.36
  159.6 17.6 %fusion.4 = f32[2048,1024]{0,1:T(8,128)} fusion(f32[2048,8,128]{0,2,1:T(8,128)} %copy.29, bf16[2048,1024]{0,1:T(8,128)(2,1)} %bitcast.61, bf16[2048,2048]{1,0:T(8,128)(2,1)} %all-gather.5.cloned.1.call-done), kind=kOutput, calls=%fused_computation.10 | convolution fusion | flops 8596226048 | bytes 29360128 | tf_op jit(solution)/shard_map/dot_general | solution.py:39
  177.2 5.1 reduce_sum.9
  183.2 22.4 %reduce-scatter.2.cloned.1.call-done = f32[512,128]{0,1:T(8,128)} async-done(((f32[2048,128]{0,1:T(8,128)}), f32[512,128]{0,1:T(8,128)}) %reduce-scatter.2.cloned.1.call-update) | async-done | bytes 262160 | tf_op jit(solution)/shard_map/reduce_scatter | solution.py:46
  205.6 1.1 copy.32
  206.7 180.5 %gather_fusion = f32[32768]{0:T(1024)S(1)} fusion(f32[65536]{0:T(1024)S(1)} %bitcast.58, s32[32768]{0:T(1024)S(1)} %broadcast_clamp_fusion), kind=kCustom, calls=%fused_computation | custom fusion | bytes 393216 | tf_op jit(solution)/shard_map/gather | solution.py:13
  387.3 171.1 %scatter_custom_fusion = f32[65536]{0:T(1024)S(1)} fusion(s32[32768]{0:T(1024)S(1)} %bitcast.67, f32[32768]{0:T(1024)S(1)} %multiply_select_fusion, f32[]{:T(128)} %constant.3.clone.1), kind=kCustom, calls=%fused_computation.23 | custom fusion | flops 32768 | bytes 262148 | tf_op jit(solution)/shard_map/scatter-add | solution.py:18
  558.4 6.8 all_gather.11
  565.3 4.0 multiply_convert_fusion
  569.3 6.7 copy.33
  576.0 14.4 %fusion.3 = bf16[2048,1024]{0,1:T(8,128)(2,1)} fusion(bf16[2048,1024]{0,1:T(8,128)(2,1)} %bitcast.62, bf16[2048,2048]{1,0:T(8,128)(2,1)} %all-gather.5.cloned.1.call-done), kind=kOutput, calls=%fused_computation.8 | convolution fusion | flops 8596226048 | bytes 16777216 | tf_op jit(solution)/shard_map/dot_general | solution.py:59
  590.4 6.7 copy.34
  597.1 99.4 %all_to_all.30 = bf16[2048,8,128]{2,1,0:T(8,128)(2,1)S(1)} all-to-all(bf16[2048,8,128]{2,1,0:T(8,128)(2,1)} %copy.34), channel_id=1, replica_groups=mesh['mem'=4,'lon'=8] {'lon'}, dimensions={0} | all-to-all | bytes 8388608 | tf_op jit(solution)/shard_map/all_to_all | solution.py:67
  696.6 6.7 fusion.2
  (18 shorter events, 0.5 us)
Async XLA Ops:
  6.5 27.7 %all-gather.3.cloned.1.call-start = ((), (), s32[]{:S(2)}) async-start(), calls=%async_computation.3 | async-start | bytes 2621440 | tf_op jit(solution)/shard_map/all_gather | solution.py:25
  7.3 152.4 %all-gather.5.cloned.1.call-start = ((), (), s32[]{:S(2)}) async-start(), calls=%async_computation.4 | async-start | bytes 10485760 | tf_op jit(solution)/shard_map/all_gather | solution.py:38
  52.4 99.2 %all-to-all-start = ((bf16[256,8,1024]{0,1,2:T(8,128)(2,1)}), bf16[256,8,1024]{0,1,2:T(8,128)(2,1)}, u32[]{:S(2)}, u32[]{:S(2)}) async-start(bf16[256,8,1024]{0,1,2:T(8,128)(2,1)} %copy.30), calls=%async_computation | async-start | bytes 8388608 | tf_op jit(solution)/shard_map/all_to_all | solution.py:33
  58.0 7.9 %copy-start = (s32[1,1,32768]{2,1,0:T(1,128)S(1)}, s32[1,1,32768]{2,1,0:T(1,128)}, u32[]{:S(2)}) copy-start(s32[1,1,32768]{2,1,0:T(1,128)} %param.11) | copy-start | bytes 393220
  58.0 147.6 %reduce-scatter.2.cloned.1.call-start = ((), (), s32[]{:S(2)}) async-start(), calls=%async_computation.5 | async-start | bytes 1310720 | tf_op jit(solution)/shard_map/reduce_scatter | solution.py:46
  206.7 180.6 %copy-start.1 = (f32[1,1,32768]{2,1,0:T(1,128)S(1)}, f32[1,1,32768]{2,1,0:T(1,128)}, u32[]{:S(2)}) copy-start(f32[1,1,32768]{2,1,0:T(1,128)} %param.12) | copy-start | bytes 393220
  597.1 99.4 %copy-start.2 = (bf16[256,8,1024]{2,1,0:T(8,128)(2,1)S(1)}, bf16[256,8,1024]{2,1,0:T(8,128)(2,1)}, u32[]{:S(2)}) copy-start(bf16[256,8,1024]{2,1,0:T(8,128)(2,1)} %param.7) | copy-start | bytes 12582916
  597.1 99.4 %copy-start.3 = (bf16[1024,1024]{1,0:T(8,128)(2,1)S(1)}, bf16[1024,1024]{1,0:T(8,128)(2,1)}, u32[]{:S(2)}) copy-start(bf16[1024,1024]{1,0:T(8,128)(2,1)} %all-gather.3.cloned.1.call-done) | copy-start | bytes 6291460
Sparse Core Ops, SparseCore 0:
  8.9 25.2 all-gather.2
  35.8 58.2 all-gather.4
  182.5 23.0 reduce-scatter.1
where the time goes:
time: 711 us; the launch traced here: 710 us
  local copies, waits for them, and re-layouts  218 us (31%)
  other arithmetic  181 us (25%)
  waiting for transfers between devices  136 us (19%)
  blocking collectives  106 us (15%)
  matrix products  49.4 us (7%)
  between operations  13.8 us (2%)
    gather x1, local copies, waits for them, and re-layouts, observe(): picked = flattened[where_at]  181 us
    scatter-add x1, other arithmetic, observe(): return jnp.zeros_like(flattened).at[where_at.reshape(-1)].add(values.resh...  171 us
    all_to_all x1, blocking collectives, local(): lax.all_to_all(spread, 'lon', split_axis=0, concat_axis=2, tiled=True)  99.4 us
    all_to_all x1, waiting for transfers between devices, local(): lax.all_to_all(banded.reshape(lon_dev, mem_dev, lat_all), 'lon', split_ax...  85.6 us
    all_gather x1, waiting for transfers between devices, local(): lat_full = lax.all_gather(lat_factor, 'mem', axis=0, tiled=True)  26.2 us
    reduce_scatter x1, waiting for transfers between devices, local(): lax.psum_scatter(partial_sum, 'mem', scatter_dimension=0, tiled=True)  22.4 us
    dot_general x1, matrix products, local(): spread_fwd = jnp.dot(lon_full, columns, preferred_element_type=jnp.float32)  17.6 us
    dot_general x1, matrix products, local(): lax.dot_general(lon_full, weighted, (((0,), (0,)), ((), ())), preferred_e...  14.4 us
  transfers between devices with their start and end apart: 4, of which 3 were waited for; matrix products, arithmetic and copies ran while one was open for 5% of the time, Pallas kernels for 0%

commit v1 on v0

--- a/solution.py
+++ b/solution.py
@@ -30,8 +30,16 @@
             control_rows, lat_full, (((1,), (1,)), ((), ())), preferred_element_type=jnp.float32
         )
     ).astype(jnp.bfloat16)
-    moved = lax.all_to_all(
-        banded.reshape(lon_dev, mem_dev, lat_all), "lon", split_axis=2, concat_axis=0, tiled=True
+    moved = jnp.concatenate(
+        lax.all_to_all(
+            jnp.stack(
+                jnp.split(banded.reshape(lon_dev, mem_dev, lat_all), lax.axis_size("lon"), axis=2)
+            ),
+            "lon",
+            0,
+            0,
+        ),
+        axis=0,
     )
     lon_all, _, lat_band = moved.shape
     columns = moved.reshape(lon_all, mem_dev * lat_band)

time: 711 us -> 712 us (level)
    unnamed x9 -> x16, local copies, waits for them, and re-layouts: 3.42 us -> 11.9 us
    reshape x1 -> x0, local copies, waits for them, and re-layouts: 7.47 us -> none  [local(): banded.reshape(lon_dev, mem_dev, lat_all)]
    another operation x0 -> x2, local copies, waits for them, and re-layouts: none -> 7.46 us  [the longest x1 6.51 us: local(): columns = moved.reshape(lon_all, mem_dev * lat_band)]
where the time goes in v1:
time: 712 us; the launch traced here: 711 us
  local copies, waits for them, and re-layouts  222 us (31%)
  other arithmetic  181 us (25%)
  waiting for transfers between devices  135 us (19%)
  blocking collectives  106 us (15%)
  matrix products  47.3 us (7%)
  between operations  13.9 us (2%)
    gather x1, local copies, waits for them, and re-layouts, observe(): picked = flattened[where_at]  181 us
    scatter-add x1, other arithmetic, observe(): return jnp.zeros_like(flattened).at[where_at.reshape(-1)].add(values.resh...  171 us
    all_to_all x1, blocking collectives, local(): lax.all_to_all(spread, 'lon', split_axis=0, concat_axis=2, tiled=True)  99.4 us
    all_to_all x1, waiting for transfers between devices, local(): lax.all_to_all(jnp.stack(jnp.split(banded.reshape(lon_dev, mem_dev, lat_a...  85.6 us
    all_gather x1, waiting for transfers between devices, local(): lat_full = lax.all_gather(lat_factor, 'mem', axis=0, tiled=True)  26.2 us
    reduce_scatter x1, waiting for transfers between devices, local(): lax.psum_scatter(partial_sum, 'mem', scatter_dimension=0, tiled=True)  22.2 us
    dot_general x1, matrix products, local(): spread_fwd = jnp.dot(lon_full, columns, preferred_element_type=jnp.float32)  17.6 us
    dot_general x1, matrix products, local(): lax.dot_general(lon_full, weighted, (((0,), (0,)), ((), ())), preferred_e...  14.4 us
  transfers between devices with their start and end apart: 4, of which 3 were waited for; matrix products, arithmetic and copies ran while one was open for 5% of the time, Pallas kernels for 0%

profile of v1, /device:TPU:0, one launch (start us, length us, event | category | flops | bytes accessed | tf_op | source)
XLA Modules:
  0.0 711.4 jit_solution(10434496759606298323)
XLA Ops:
  8.0 26.2 %all-gather.3.cloned.1.call-done = bf16[1024,1024]{1,0:T(8,128)(2,1)} async-done(((bf16[256,1024]{1,0:T(8,128)(2,1)}), bf16[1024,1024]{1,0:T(8,128)(2,1)}) %all-gather.3.cloned.1.call-update) | async-done | bytes 2097168 | tf_op jit(solution)/shard_map/all_gather | solution.py:25
  34.2 8.6 %fusion.5 = bf16[256,8,1024]{2,1,0:T(8,128)(2,1)S(1)} fusion(bf16[256,8,1024]{2,1,0:T(8,128)(2,1)} %param.7, bf16[1024,1024]{1,0:T(8,128)(2,1)} %all-gather.3.cloned.1.call-done), kind=kOutput, calls=%fused_computation.12 | convolution fusion | flops 4301258752 | bytes 10485760 | tf_op jit(solution)/shard_map/dot_general | solution.py:29
  42.8 1.0 fusion.22
  43.8 1.0 fusion.21
  46.6 1.0 fusion.18
  49.4 0.9 fusion.15
  50.4 5.5 all-to-all-start
  56.1 7.7 %copy.21 = f32[2048,8,128]{0,2,1:T(8,128)} copy(bf16[2048,8,128]{2,1,0:T(8,128)(2,1)} %param.8) | data formatting | bytes 12582912 | tf_op jit(solution)/shard_map/convert_element_type | solution.py:63
  63.9 85.6 %all-to-all-done = bf16[8,256,8,128]{3,2,1,0:T(8,128)(2,1)} async-done(((bf16[8,256,8,128]{3,2,1,0:T(8,128)(2,1)}), bf16[8,256,8,128]{3,2,1,0:T(8,128)(2,1)}, u32[]{:S(2)}, u32[]{:S(2)}) %all-to-all-start) | async-done | bytes 4194336 | tf_op jit(solution)/shard_map/all_to_all | solution.py:34
  149.6 5.2 copy.38
  154.8 6.5 copy.27
  161.3 17.6 %fusion.4 = f32[2048,1024]{0,1:T(8,128)} fusion(f32[2048,8,128]{0,2,1:T(8,128)} %copy.21, bf16[2048,1024]{0,1:T(8,128)(2,1)} %copy.27, bf16[2048,2048]{1,0:T(8,128)(2,1)} %all-gather.5.cloned.1.call-done, bf16[256,8,8,128]{3,2,1,0:T(8,128)(2,1)} %bitcast.30), kind=kOutput, calls=%fused_computation.10 | convolution fusion | flops 8596226048 | bytes 33554432 | tf_op jit(solution)/shard_map/dot_general | solution.py:47
  179.0 5.1 reduce_sum.9
  185.0 22.2 %reduce-scatter.2.cloned.1.call-done = f32[512,128]{0,1:T(8,128)} async-done(((f32[2048,128]{0,1:T(8,128)}), f32[512,128]{0,1:T(8,128)}) %reduce-scatter.2.cloned.1.call-update) | async-done | bytes 262160 | tf_op jit(solution)/shard_map/reduce_scatter | solution.py:54
  207.2 1.1 copy.23
  208.3 180.5 %gather_fusion = f32[32768]{0:T(1024)S(1)} fusion(f32[65536]{0:T(1024)S(1)} %bitcast.88, s32[32768]{0:T(1024)S(1)} %broadcast_clamp_fusion), kind=kCustom, calls=%fused_computation | custom fusion | bytes 393216 | tf_op jit(solution)/shard_map/gather | solution.py:13
  388.9 171.1 %scatter_custom_fusion = f32[65536]{0:T(1024)S(1)} fusion(s32[32768]{0:T(1024)S(1)} %bitcast.96, f32[32768]{0:T(1024)S(1)} %multiply_select_fusion, f32[]{:T(128)} %constant.3.clone.1), kind=kCustom, calls=%fused_computation.40 | custom fusion | flops 32768 | bytes 262148 | tf_op jit(solution)/shard_map/scatter-add | solution.py:18
  560.0 6.8 all_gather.11
  566.9 4.0 multiply_convert_fusion
  570.9 6.7 copy.24
  577.6 14.4 %fusion.3 = bf16[2048,1024]{0,1:T(8,128)(2,1)} fusion(bf16[2048,1024]{0,1:T(8,128)(2,1)} %bitcast.91, bf16[2048,2048]{1,0:T(8,128)(2,1)} %all-gather.5.cloned.1.call-done), kind=kOutput, calls=%fused_computation.8 | convolution fusion | flops 8596226048 | bytes 16777216 | tf_op jit(solution)/shard_map/dot_general | solution.py:67
  592.0 6.7 copy.25
  598.7 99.4 %all_to_all.20 = bf16[2048,8,128]{2,1,0:T(8,128)(2,1)S(1)} all-to-all(bf16[2048,8,128]{2,1,0:T(8,128)(2,1)} %copy.25), channel_id=1, replica_groups=mesh['mem'=4,'lon'=8] {'lon'}, dimensions={0} | all-to-all | bytes 8388608 | tf_op jit(solution)/shard_map/all_to_all | solution.py:75
  698.2 6.7 fusion.2
  (25 shorter events, 5.8 us)
Async XLA Ops:
  6.5 27.7 %all-gather.3.cloned.1.call-start = ((), (), s32[]{:S(2)}) async-start(), calls=%async_computation.3 | async-start | bytes 2621440 | tf_op jit(solution)/shard_map/all_gather | solution.py:25
  7.3 154.1 %all-gather.5.cloned.1.call-start = ((), (), s32[]{:S(2)}) async-start(), calls=%async_computation.4 | async-start | bytes 10485760 | tf_op jit(solution)/shard_map/all_gather | solution.py:46
  50.4 99.2 %all-to-all-start = ((bf16[8,256,8,128]{3,2,1,0:T(8,128)(2,1)}), bf16[8,256,8,128]{3,2,1,0:T(8,128)(2,1)}, u32[]{:S(2)}, u32[]{:S(2)}) async-start(bf16[8,256,8,128]{3,2,1,0:T(8,128)(2,1)} %fusion.15), calls=%async_computation | async-start | bytes 8388608 | tf_op jit(solution)/shard_map/all_to_all | solution.py:34
  55.9 7.9 %copy-start = (s32[1,1,32768]{2,1,0:T(1,128)S(1)}, s32[1,1,32768]{2,1,0:T(1,128)}, u32[]{:S(2)}) copy-start(s32[1,1,32768]{2,1,0:T(1,128)} %param.11) | copy-start | bytes 393220
  55.9 151.3 %reduce-scatter.2.cloned.1.call-start = ((), (), s32[]{:S(2)}) async-start(), calls=%async_computation.5 | async-start | bytes 1310720 | tf_op jit(solution)/shard_map/reduce_scatter | solution.py:54
  208.3 180.6 %copy-start.1 = (f32[1,1,32768]{2,1,0:T(1,128)S(1)}, f32[1,1,32768]{2,1,0:T(1,128)}, u32[]{:S(2)}) copy-start(f32[1,1,32768]{2,1,0:T(1,128)} %param.12) | copy-start | bytes 393220
  598.7 99.4 %copy-start.2 = (bf16[256,8,1024]{2,1,0:T(8,128)(2,1)S(1)}, bf16[256,8,1024]{2,1,0:T(8,128)(2,1)}, u32[]{:S(2)}) copy-start(bf16[256,8,1024]{2,1,0:T(8,128)(2,1)} %param.7) | copy-start | bytes 12582916
  598.7 99.4 %copy-start.3 = (bf16[1024,1024]{1,0:T(8,128)(2,1)S(1)}, bf16[1024,1024]{1,0:T(8,128)(2,1)}, u32[]{:S(2)}) copy-start(bf16[1024,1024]{1,0:T(8,128)(2,1)} %all-gather.3.cloned.1.call-done) | copy-start | bytes 6291460
Sparse Core Ops, SparseCore 0:
  8.9 25.2 all-gather.2
  35.8 58.2 all-gather.4
  184.3 22.9 reduce-scatter.1
